TPU v7x, 32 devices: a whole 2x2x4 slice. The times are simulated.
32 devices in a mesh: head: 4 (over z), node: 8 (over y, x, core).
Axes of the slice: x: 2, y: 2, z: 4, core: 2. Of those that a mesh axis runs over, the one named last changes fastest.
Arguments:
- node_input: bfloat16 [8192, 512], P('node'), may hold values from -6 to 6
- cotangent: bfloat16 [8192, 512], P('node'), may hold values from -6 to 6
- sigma_embed: bfloat16 [4, 512], replicated, may hold values from -5 to 5
- neighbours: int32 [8192, 16], P('node'), may hold values from 0 to 8191, as said below
- neighbour_valid: int32 [8192, 16], P('node'), may hold values 0 or 1
- batch_counts: int32 [4], replicated, may hold values from 1 to 4096, 8192 in all
- step_count: int32 [1], replicated, may hold values from 1 to 20
- ada_master: float32 [512, 2048], P('node'), may hold values from -0.125 to 0.125
- ada_first: float32 [512, 2048], P('node'), may hold values from -768 to 768
- ada_second: float32 [512, 2048], P('node'), may hold values from 16384 to 65536
- qkv_master: float32 [512, 1536], P('node', 'head'), may hold values from -0.375 to 0.375
- qkv_first: float32 [512, 1536], P('node', 'head'), may hold values from -1024 to 1024
- qkv_second: float32 [512, 1536], P('node', 'head'), may hold values from 32768 to 131072
- out_master: float32 [512, 512], P(('head', 'node')), may hold values from -0.5 to 0.5
- out_first: float32 [512, 512], P(('head', 'node')), may hold values from -384 to 384
- out_second: float32 [512, 512], P(('head', 'node')), may hold values from 4096 to 16384
- up_master: float32 [512, 2048], P('node', 'head'), may hold values from -0.25 to 0.25
- up_first: float32 [512, 2048], P('node', 'head'), may hold values from -128 to 128
- up_second: float32 [512, 2048], P('node', 'head'), may hold values from 491.52 to 2048
- down_master: float32 [2048, 512], P(('head', 'node')), may hold values from -0.125 to 0.125
- down_first: float32 [2048, 512], P(('head', 'node')), may hold values from -256 to 256
- down_second: float32 [2048, 512], P(('head', 'node')), may hold values from 2048 to 8192
Outputs:
- node_output: bfloat16 [8192, 512], P('node')
- input_grad: float32 [8192, 512], P('node')
- ada_new: float32 [512, 2048], P('node')
- ada_first_new: float32 [512, 2048], P('node')
- ada_second_new: float32 [512, 2048], P('node')
- qkv_new: float32 [512, 1536], P('node', 'head')
- qkv_first_new: float32 [512, 1536], P('node', 'head')
- qkv_second_new: float32 [512, 1536], P('node', 'head')
- out_new: float32 [512, 512], P(('head', 'node'))
- out_first_new: float32 [512, 512], P(('head', 'node'))
- out_second_new: float32 [512, 512], P(('head', 'node'))
- up_new: float32 [512, 2048], P('node', 'head')
- up_first_new: float32 [512, 2048], P('node', 'head')
- up_second_new: float32 [512, 2048], P('node', 'head')
- down_new: float32 [2048, 512], P(('head', 'node'))
- down_first_new: float32 [2048, 512], P(('head', 'node'))
- down_second_new: float32 [2048, 512], P(('head', 'node'))
Inputs may be any that keep to these rules, and one draw needn't show every extreme that they name: `batch_counts`: the counts sum to 8192; the largest is exactly 4096. Node n's neighbours lie in its own aligned block of 1024 nodes or in the two blocks on either side of it, counted cyclically over the 8192 nodes.
All inputs are finite; a program needn't handle non-finite values. No bound on the sum of `neighbour_valid` on one device may be relied on, other than what follows from the above.
Results may differ from a plain program's by a relative error of at most 0.018.
The roundings to bfloat16 on the way count: a program that leaves them out, or rounds other values in their place, can miss the bound.
Values may be sent and summed in bfloat16 or wider, within the bound.
A program may use at most 128 MiB of HBM per device.

v0:
```python
import functools
import math

import jax
import jax.numpy as jnp
from jax import lax
from jax.experimental import pallas as pl
from jax.experimental.pallas import tpu as pltpu
from jax.sharding import PartitionSpec as P


WIDTH = 512
HIDDEN_SIZE = 2048
COND = 512


norm_eps = 1e-06
beta_rate = 0.5
adam_eps = 1e-08
weight_decay = 0.1
highest = lax.Precision.HIGHEST


def passed_along(block, axis, distance):
    devices = range(lax.axis_size(axis))
    route = [((i - distance) % len(devices), i) for i in devices]
    return lax.ppermute(block, axis, route)


def norm_parts(values):
    centred = values - jnp.mean(values, axis=1, keepdims=True)
    inverse = lax.rsqrt(jnp.mean(centred * centred, axis=1, keepdims=True) + norm_eps)
    return (centred * inverse, inverse)


def norm_back(grad_normed, normed, inverse):
    first_mean = jnp.mean(grad_normed, axis=1, keepdims=True)
    second_mean = jnp.mean(grad_normed * normed, axis=1, keepdims=True)
    return inverse * (grad_normed - first_mean - normed * second_mean)


def adamw_update(master, first, second, grad, rate, count_value):
    first_new = beta_rate * first + (1.0 - beta_rate) * grad
    second_new = beta_rate * second + (1.0 - beta_rate) * grad * grad
    correct = 1.0 - jnp.power(jnp.float32(beta_rate), count_value)
    normed_step = first_new / correct / (jnp.sqrt(second_new / correct) + adam_eps)
    master_new = master - rate * (normed_step + weight_decay * master)
    return (master_new, first_new, second_new)


f32=jnp.float32; bf16=jnp.bfloat16
NT=(((1,),(1,)),((),()))
SPAN=256

def count_groups(cnt, code, rows, start, stop, step):
    parts=rows//SPAN
    total=5*parts*16
    short=jnp.int16
    rowid=lax.broadcasted_iota(jnp.int32,(total,SPAN),0).astype(short)
    spot=lax.broadcasted_iota(jnp.int32,(SPAN,SPAN),0).astype(short)
    one=bf16(1); zero=bf16(0)
    def group(g):
        both=code[pl.ds(g,1),:]
        keys=lax.shift_right_arithmetic(both,8).astype(short)
        low=lax.bitwise_and(both,255).astype(short)
        left=jnp.where(rowid==jnp.broadcast_to(keys,(total,SPAN)),one,zero)
        right=jnp.where(spot==jnp.broadcast_to(low,(SPAN,SPAN)),one,zero)
        made=lax.dot_general(left,right,NT,preferred_element_type=f32).astype(bf16)
        at=pl.multiple_of(g*16,16)
        for b in range(5):
            for p in range(parts):
                r=(b*parts+p)*16
                cnt[b,pl.ds(at,16),p*SPAN:(p+1)*SPAN]=made[r:r+16,:]
    def body(g,_):
        for u in range(step): group(g*step+u)
        return 0
    lax.fori_loop(start//step,stop//step,body,0)

def add_self(cnt, block, rows):
    eye=(lax.broadcasted_iota(jnp.int32,(SPAN,SPAN),0)==lax.broadcasted_iota(jnp.int32,(SPAN,SPAN),1))
    one=jnp.where(eye,1.0,0.0).astype(bf16)
    for p in range(rows//SPAN):
        s=slice(p*SPAN,(p+1)*SPAN)
        cnt[block,s,s]=cnt[block,s,s]+one

def attend_rows(b, first, at, q, table, e, m, l, acc, fac, scale):
    size=at.stop-at.start
    lane=lax.broadcasted_iota(jnp.int32,(size,128),1)
    s=lax.dot_general(q[at,:],table[b,:,0:128],NT,preferred_element_type=f32)*scale
    c=e[b,at,:].astype(f32)
    s=jnp.where(c>0,s,-1e30)
    top=jnp.max(s,axis=1,keepdims=True)
    if not first:
        old=m[at,0:1]
        top=jnp.maximum(top,old)
    w=(jnp.exp2(s-top)*c).astype(bf16)
    e[b,at,:]=w
    out=jnp.dot(w,table[b,:,128:384],preferred_element_type=f32)
    if first:
        acc[at,:]=out[:,:128]; l[at,:]=out[:,128:]
        fac[at,:]=jnp.where(lane==b,top,0.0)
    else:
        shrink=jnp.exp2(old-top)
        acc[at,:]=acc[at,:]*shrink+out[:,:128]
        l[at,:]=l[at,:]*shrink+out[:,128:]
        fac[at,:]=jnp.where(lane==b,top,fac[at,:])
    m[at,:]=jnp.broadcast_to(top,(size,128))

def back_block(b, q_t, dof, fac, delta, table, e, dq, write, first, chunk, keyscale):
    rows=dof.shape[0]
    f=fac[:,b:b+1]
    dobh=(dof*f).astype(bf16)
    d=-(delta*f)
    h=d.astype(bf16); r=d-h.astype(f32); h2=r.astype(bf16); h3=(r-h2.astype(f32)).astype(bf16)
    lane=lax.broadcasted_iota(jnp.int32,(rows,128),1)
    dcol=jnp.where(lane==0,h.astype(f32),jnp.where(lane==1,h2.astype(f32),jnp.where(lane==2,h3.astype(f32),0.0))).astype(bf16)
    left=jnp.concatenate([dobh,dcol],axis=1)
    dob_t=dobh.T
    for i in range(rows//chunk):
        s=slice(i*chunk,(i+1)*chunk)
        dp=lax.dot_general(left,table[b,s,128:384],NT,preferred_element_type=f32)
        w=e[b,:,s]
        ds=(dp*w.astype(f32)).astype(bf16)
        write(slice(0,128),s,jnp.dot(q_t,ds,preferred_element_type=f32)*keyscale)
        write(slice(128,256),s,jnp.dot(dob_t,w,preferred_element_type=f32))
        out=jnp.dot(ds,table[b,s,0:128],preferred_element_type=f32)
        if first and i==0: dq[...]=out
        else: dq[...]+=out


def by_batch(pos, limits, table, row, lanes):
    pick=[table[row+b:row+b+1,lanes] for b in range(4)]
    out=jnp.where(pos>=limits[0],pick[1],pick[0])
    out=jnp.where(pos>=limits[1],pick[2],out)
    return jnp.where(pos>=limits[2],pick[3],out)


def batch_sums(pos, limits, values):
    lane=lax.broadcasted_iota(jnp.int32,(pos.shape[0],8),1)
    member=(pos>=limits[0]).astype(jnp.int32)+(pos>=limits[1]).astype(jnp.int32)+(pos>=limits[2]).astype(jnp.int32)
    onehot=jnp.where(lane==member,1.0,0.0).astype(f32)
    return lax.dot_general(onehot,values,(((0,),(0,)),((),())),precision=highest,preferred_element_type=f32)[0:4,:]


class Links:
    def __init__(self, send, recv):
        self.send, self.recv, self.used = send, recv, 0

    def copy(self, src, dst, head, node):
        made=pltpu.make_async_remote_copy(src_ref=src,dst_ref=dst,send_sem=self.send.at[self.used],recv_sem=self.recv.at[self.used],
            device_id=(head,node),device_id_type=pl.DeviceIdType.MESH)
        self.used+=1
        return made

    def go(self, src, dst, head, node):
        made=self.copy(src,dst,head,node)
        made.start()
        return made


def meet(peers):
    barrier=pltpu.get_barrier_semaphore()
    for head,node in peers:
        pl.semaphore_signal(barrier,inc=1,device_id=(head,node),device_id_type=pl.DeviceIdType.MESH)
    pl.semaphore_wait(barrier,len(peers))


def wait_all(copies):
    for c in copies: c.wait()


def block_of(index, size):
    return pl.ds(pl.multiple_of(index*size,size),size)


def summed(*refs):
    total=refs[0].astype(f32)
    for r in refs[1:]: total=total+r.astype(f32)
    return total


NAMES=("ada","qkv","out","up","down")


def scratch(rows):
    part=rows//4
    return dict(
        e=((5,rows,rows),bf16),m=((rows,128),f32),l=((rows,128),f32),att=((rows,128),f32),fac=((rows,128),f32),
        queries=((rows,128),bf16),table=((5,rows,384),bf16),xn_one=((rows,512),bf16),
        qkv_full=((512,384),bf16),out_full=((4,128,512),bf16),up_full=((512,2048),bf16),down_full=((4,512,512),bf16),
        modp=((8,1024),f32),modbuf=((8,8,1024),f32),modulation=((8,1024),f32),
        mixed=((rows,128),bf16),heads=((part,512),bf16),do=((rows,128),bf16),do_rows=((part,512),bf16),
        act=((part,2048),bf16),pre=((part,2048),bf16),dy=((part,512),f32),out_rows=((part,512),bf16),
        up_grad=((4,2,64,2048),bf16),down_grad=((4,4,2,64,512),bf16),out_grad=((4,4,2,16,512),bf16),
        dq=((rows,128),f32),dkv=((256,rows),f32),near=((5,256,rows),bf16),
        got_pair=((256,rows),bf16),got_y=((256,rows),bf16),got_x=((256,rows),bf16),got_one=((256,rows),bf16),
        proj_grad=((rows,384),bf16),partial=((4,part,512),bf16),got_partial=((3,part,512),bf16),rows_grad=((part,512),bf16),normed=((rows,512),f32),
        up1=((4,64,2048),bf16),down1=((4,4,64,512),bf16),out1=((4,4,16,512),bf16),
        up2=((2,64,2048),bf16),down2=((4,2,64,512),bf16),out2=((4,2,16,512),bf16),
        up3=((64,2048),bf16),down3=((4,64,512),bf16),out3=((4,16,512),bf16),
        up_z=((3,64,512),bf16),down_z=((3,64,512),bf16),out_z=((3,16,512),bf16),
        qkv_grad=((8,64,384),bf16),qkv_got=((7,64,384),bf16),dm_own=((8,1024),f32),dm_z=((4,8,1024),f32),dm_n=((8,8,1024),f32),
    )


class Bag:
    pass


COPIES=14+9+8+4+9+9+1+3+6+55


def layer_kernel(scale, names, *refs):
    refs=list(refs)
    take=lambda n: [refs.pop(0) for _ in range(n)]
    node_input,cotangent,sigma,code,counts=take(5)
    w={n:refs.pop(0) for n in NAMES}
    node_output,row_all,qkv_sum,out_sum,up_sum,down_sum,mod_sum=take(7)
    k=Bag()
    for n in names: setattr(k,n,refs.pop(0))
    send,recv=take(2)
    head=lax.axis_index("head"); node=lax.axis_index("node")
    y_at=node//4; x_at=(node//2)%2; core=node%2
    rows=node_input.shape[0]
    part=rows//4
    links=Links(send,recv)
    go=links.go
    normed=k.normed
    quarter=[slice(i*part,(i+1)*part) for i in range(4)]
    limits=(counts[0],counts[0]+counts[1],counts[0]+counts[1]+counts[2])
    mine=block_of(head,part)
    head_cols=block_of(head,512)
    own_pos=node*rows+head*part+lax.broadcasted_iota(jnp.int32,(part,1),0)

    own=block_of(node,64); own_out=block_of(node,16)
    k.qkv_full[own,:]=w["qkv"][...].astype(bf16)
    sig=sigma[:,0:64]
    for i in range(1,8): sig=jnp.where(node==i,sigma[:,i*64:(i+1)*64],sig)
    made=jnp.dot(sig,w["ada"][...].astype(bf16),preferred_element_type=f32)
    k.modp[0:4,:]=made[:,:1024]
    k.modp[4:8,:]=made[:,1024:]
    k.up_full[own,head_cols]=w["up"][...].astype(bf16)
    k.down_full[head,own,:]=w["down"][...].astype(bf16)
    k.out_full[head,own_out,:]=w["out"][...].astype(bf16)
    meet([(head,node^i) for i in range(1,8)]+[(head^i,node) for i in range(1,4)])
    first=[]
    for i in range(1,8):
        first.append(go(k.modp,k.modbuf.at[node],head,node^i))
        first.append(go(k.qkv_full.at[own],k.qkv_full.at[own],head,node^i))
    along=[]
    for i in range(1,4):
        for ref in (k.up_full.at[own,head_cols],k.down_full.at[head,own],k.out_full.at[head,own_out]):
            along.append(go(ref,ref,head^i,node))
    k.modbuf[node,:,:]=k.modp[...]
    for b in range(5): k.table[b,:,256:384]=jnp.ones((rows,128),bf16)
    def norm(i,_):
        at=block_of(i,256)
        v=node_input[at,:].astype(f32)
        centred=v-jnp.mean(v,axis=1,keepdims=True)
        normed[at,:]=centred*lax.rsqrt(jnp.mean(centred*centred,axis=1,keepdims=True)+norm_eps)
        return 0
    lax.fori_loop(0,rows//256,norm,0)
    groups=code.shape[0]
    half=groups//2
    count_groups(k.e,code,rows,0,half,8)
    wait_all(first)
    mod=k.modbuf[0]
    for i in range(1,8): mod=mod+k.modbuf[i]
    k.modulation[...]=mod

    kv=slice(0,256)
    across=[]; paired=[]
    for at in quarter:
        pos=node*rows+at.start+lax.broadcasted_iota(jnp.int32,(part,1),0)
        xn=(normed[at,:]*(1.0+by_batch(pos,limits,k.modulation,0,slice(0,512)))+by_batch(pos,limits,k.modulation,0,slice(512,1024))).astype(bf16)
        k.xn_one[at,:]=xn
        proj=jnp.dot(xn,k.qkv_full[...],preferred_element_type=f32).astype(bf16)
        k.queries[at,:]=proj[:,:128]
        k.table[0,at,kv]=proj[:,128:]
        across.append(go(k.table.at[0,at,kv],k.table.at[2,at,kv],head,node^2))
        paired.append(go(k.table.at[0,at,kv],k.table.at[1,at,kv],head,node^1))
    count_groups(k.e,code,rows,half,groups,8)
    add_self(k.e,0,rows)

    onward=[]
    def pass_keys(i):
        at=quarter[i]
        across[i].wait_recv()
        onward.append(go(k.table.at[2,at,kv],k.table.at[3,at,kv],head,node^4))
    def attend(b,at):
        attend_rows(b,b==0,at,k.queries,k.table,k.e,k.m,k.l,k.att,k.fac,scale*math.log2(math.e))
    def column(which):
        at=block_of(node^which,64)
        return [k.up_full.at[at],k.down_full.at[:,at],k.out_full.at[:,block_of(node^which,16)]]
    pass_keys(0)
    for at in quarter: attend(0,at)
    pass_keys(1)
    wait_all(paired)
    for at in quarter: attend(1,at)
    pass_keys(2)
    pass_keys(3)
    wait_all(along)
    own_column=column(0)
    to_x=[go(r,r,head,node^2) for r in own_column]
    to_y=[go(r,r,head,node^4) for r in own_column]
    to_pair=[go(r,r,head,node^1) for r in own_column]
    for at in quarter: attend(2,at)
    wait_all(onward)
    fifth=go(k.table.at[jnp.where(x_at==core,2,3),:,kv],k.table.at[4,:,kv],head,node^1)
    for at in quarter: attend(3,at)
    fifth.wait()
    lanes=block_of(head,128)
    moved=[]
    for i in range(4):
        at=quarter[i]
        attend(4,at)
        inv=1.0/k.l[at,:]
        o=k.att[at,:]*inv
        k.att[at,:]=o
        k.fac[at,:]=jnp.exp2(k.fac[at,:]-k.m[at,:])*inv
        k.mixed[at,:]=o.astype(bf16)
    for i in range(1,4):
        moved.append(go(k.mixed.at[block_of(head^i,part)],k.heads.at[:,lanes],head^i,node))
    k.heads[:,lanes]=k.mixed[mine,:]
    for c in across: c.wait_send()
    wait_all(to_x+to_y)
    from_x=column(2); from_y=column(4)
    cross=[go(from_x[0],from_x[0],head,node^4)]+[go(r,r,head,node^2) for r in from_y[1:]]
    hand=[go(r,r,head,node^1) for r in from_x+from_y]
    wait_all(cross)
    last=[go(r,r,head,node^1) for r in column(6)]
    scale_two=1.0+by_batch(own_pos,limits,k.modulation,4,slice(0,512))
    shift_two=by_batch(own_pos,limits,k.modulation,4,slice(512,1024))
    g=cotangent[mine,:]
    wait_all(moved)
    wait_all(to_pair+hand+last)

    out_all=k.out_full[...].reshape(512,512)
    y=node_input[mine,:].astype(f32)+jnp.dot(k.heads[...],out_all,preferred_element_type=f32)
    n_two,inv_two=norm_parts(y)
    xn=(n_two*scale_two+shift_two).astype(bf16)
    mlp=jnp.zeros((part,512),f32); dxn=jnp.zeros((part,512),f32)
    for j in range(4):
        s=slice(j*512,(j+1)*512)
        h=jnp.dot(xn,k.up_full[:,s],preferred_element_type=f32)
        gate=1.0/(1.0+jnp.exp(-h))
        u=(h*gate).astype(bf16)
        k.act[:,s]=u
        mlp+=jnp.dot(u,k.down_full[j],preferred_element_type=f32)
        du=lax.dot_general(g,k.down_full[j],NT,preferred_element_type=f32)
        d=(du*gate*(1.0+h*(1.0-gate))).astype(bf16)
        k.pre[:,s]=d
        dxn+=lax.dot_general(d,k.up_full[:,s],NT,preferred_element_type=f32)
    dyv=g.astype(f32)+norm_back(dxn*scale_two,n_two,inv_two)
    k.dy[...]=dyv
    da=dyv.astype(bf16)
    k.do_rows[...]=lax.dot_general(da,out_all,NT,preferred_element_type=f32).astype(bf16)
    returned=[]
    for i in range(1,4):
        returned.append(go(k.do_rows.at[:,block_of(head^i,128)],k.do.at[mine],head^i,node))
    k.do[mine,:]=k.do_rows[:,lanes]
    k.out_rows[...]=(y+mlp).astype(bf16)
    xn_t=xn.T
    heads_t=k.heads[...].T
    k.out_grad[...]=jnp.dot(heads_t,da,preferred_element_type=f32).astype(bf16).reshape(4,4,2,16,512)
    for j in range(4):
        s=slice(j*512,(j+1)*512)
        k.up_grad[:,:,:,s]=jnp.dot(xn_t,k.pre[:,s],preferred_element_type=f32).astype(bf16).reshape(4,2,64,512)
        k.down_grad[j]=jnp.dot(k.act[:,s].T,g,preferred_element_type=f32).astype(bf16).reshape(4,2,64,512)
    stage1=[go(k.up_grad.at[:,1-core],k.up1,head,node^1),go(k.down_grad.at[:,:,1-core],k.down1,head,node^1),go(k.out_grad.at[:,:,1-core],k.out1,head,node^1)]
    k.dm_own[4:8,0:512]=batch_sums(own_pos,limits,dxn*n_two)
    k.dm_own[4:8,512:1024]=batch_sums(own_pos,limits,dxn)
    wait_all(returned)
    shown=[go(k.out_rows,node_output.at[mine],head^i,node) for i in range(1,4)]
    node_output[mine,:]=k.out_rows[...]

    q_t=k.queries[...].T
    dof=k.do[...].astype(f32)
    delta=jnp.sum(dof*k.att[...],axis=1,keepdims=True)
    def block(b):
        def write(r,s,v):
            if b==0: k.dkv[r,s]=v
            else: k.near[b,r,s]=v.astype(bf16)
        back_block(b,q_t,dof,k.fac,delta,k.table,k.e,k.dq,write,b==4,512,scale)
    near=k.near
    block(4)
    give=go(near.at[4],k.got_pair,head,node^1)
    block(3)
    give.wait()
    @pl.when(x_at!=core)
    def _(): near[3]=summed(near[3],k.got_pair[...]).astype(bf16)
    via_y=[go(near.at[3,:,s],k.got_y.at[:,s],head,node^4) for s in quarter]
    block(2)
    @pl.when(x_at==core)
    def _(): near[2]=summed(near[2],k.got_pair[...]).astype(bf16)
    via_x=[]
    def pass_on(i):
        s=quarter[i]
        via_y[i].wait()
        near[2,:,s]=summed(near[2,:,s],k.got_y[:,s]).astype(bf16)
        via_x.append(go(near.at[2,:,s],k.got_x.at[:,s],head,node^2))
    pass_on(0)
    block(1)
    one=go(near.at[1],k.got_one,head,node^1)
    pass_on(1)
    pass_on(2)
    block(0)
    pass_on(3)
    wait_all(stage1)
    for i in range(4):
        k.up1[i]=summed(k.up1[i],k.up_grad[i,core]).astype(bf16)
        k.down1[i]=summed(k.down1[i],k.down_grad[i,:,core]).astype(bf16)
        k.out1[i]=summed(k.out1[i],k.out_grad[i,:,core]).astype(bf16)
    stage2=[go(k.up1.at[i*2+1-x_at],k.up2.at[i],head,node^2) for i in range(2)]
    there=pl.ds((1-y_at)*2,2)
    stage2+=[go(k.down1.at[:,there],k.down2,head,node^4),go(k.out1.at[:,there],k.out2,head,node^4)]
    xn_t=k.xn_one[...].T
    one.wait()
    for i in range(4):
        s=quarter[i]
        via_x[i].wait()
        total=k.dkv[:,s]+k.got_one[:,s].astype(f32)+k.got_x[:,s].astype(f32)
        k.proj_grad[s,128:]=total.T.astype(bf16)
        k.proj_grad[s,:128]=(k.dq[s,:]*scale).astype(bf16)
        k.partial[i]=lax.dot_general(k.proj_grad[s,:],k.qkv_full[...],NT,preferred_element_type=f32).astype(bf16)
    reduce=[go(k.partial.at[head^i],k.got_partial.at[i-1],head^i,node) for i in range(1,4)]
    k.qkv_grad[...]=jnp.dot(xn_t,k.proj_grad[...],preferred_element_type=f32).astype(bf16).reshape(8,64,384)
    qkv_moves=[go(k.qkv_grad.at[node^i],k.qkv_got.at[i-1],head,node^i) for i in range(1,8)]
    wait_all(stage2)
    for i in range(2):
        k.up2[i]=summed(k.up2[i],k.up1[i*2+x_at]).astype(bf16)
    here=pl.ds(y_at*2,2)
    k.down2[...]=summed(k.down2[...],k.down1[:,here]).astype(bf16)
    k.out2[...]=summed(k.out2[...],k.out1[:,here]).astype(bf16)
    stage3=[go(k.up2.at[1-y_at],k.up3,head,node^4),go(k.down2.at[:,1-x_at],k.down3,head,node^2),go(k.out2.at[:,1-x_at],k.out3,head,node^2)]
    scale_one=1.0+by_batch(own_pos,limits,k.modulation,0,slice(0,512))
    n_one,inv_one=norm_parts(node_input[mine,:].astype(f32))
    wait_all(qkv_moves)
    qkv_sum[...]=summed(k.qkv_grad[node],*[k.qkv_got[i] for i in range(7)])
    wait_all(stage3)
    k.up3[...]=summed(k.up3[...],k.up2[y_at]).astype(bf16)
    k.down3[...]=summed(k.down3[...],k.down2[:,x_at]).astype(bf16)
    k.out3[...]=summed(k.out3[...],k.out2[:,x_at]).astype(bf16)
    wait_all(reduce)
    dxn=summed(k.partial[head],*[k.got_partial[i] for i in range(3)])
    k.rows_grad[...]=(k.dy[...]+norm_back(dxn*scale_one,n_one,inv_one)).astype(bf16)
    spread=[go(k.rows_grad,row_all.at[head],head^i,node) for i in range(1,4)]
    row_all[head,:,:]=k.rows_grad[...]
    k.dm_own[0:4,0:512]=batch_sums(own_pos,limits,dxn*n_one)
    k.dm_own[0:4,512:1024]=batch_sums(own_pos,limits,dxn)
    dm_moves=[go(k.dm_own,k.dm_z.at[head],head^i,node) for i in range(1,4)]
    k.dm_z[head,:,:]=k.dm_own[...]
    stage4=[]
    for i in range(1,4):
        stage4+=[go(k.up3.at[:,block_of(head^i,512)],k.up_z.at[i-1],head^i,node),go(k.down3.at[head^i],k.down_z.at[i-1],head^i,node),go(k.out3.at[head^i],k.out_z.at[i-1],head^i,node)]
    wait_all(dm_moves)
    k.modp[...]=k.dm_z[0]+k.dm_z[1]+k.dm_z[2]+k.dm_z[3]
    dm_last=[go(k.modp,k.dm_n.at[node],head,node^i) for i in range(1,8)]
    k.dm_n[node,:,:]=k.modp[...]
    wait_all(dm_last)
    total=k.dm_n[0]
    for i in range(1,8): total=total+k.dm_n[i]
    mod_sum[...]=total
    wait_all(stage4)
    up_sum[...]=summed(k.up3[:,head_cols],*[k.up_z[i] for i in range(3)])
    down_sum[...]=summed(k.down3[head],*[k.down_z[i] for i in range(3)])
    out_sum[...]=summed(k.out3[head],*[k.out_z[i] for i in range(3)])
    wait_all(spread)
    wait_all(shown)


def finish_kernel(sigma, step_count, *refs):
    sources=refs[:22]; results=refs[22:39]; held=refs[39:62]; load,store=refs[62:]
    loads=[pltpu.make_async_copy(sources[i],held[i],load.at[i]) for i in range(22)]
    for i in (0,1)+tuple(range(7,22))+tuple(range(2,7)): loads[i].start()
    node=lax.axis_index("node")
    stores=[]
    def keep(ref, result):
        stores.append(pltpu.make_async_copy(ref,results[result],store.at[result])); stores[-1].start()
    loads[0].wait()
    keep(held[0],0)
    loads[1].wait()
    wide=held[22]
    rows=wide.shape[0]
    for i in range(4): wide[i*rows//4:(i+1)*rows//4,:]=held[1][i].astype(f32)
    keep(wide,1)
    count=jnp.full((8,128),step_count[0],jnp.int32).astype(f32)
    correct=(1.0-jnp.exp2(-count))[0:1,0:1]
    sig=sigma[:,0:64]
    for i in range(1,8): sig=jnp.where(node==i,sigma[:,i*64:(i+1)*64],sig)
    rates=((4*COND)**-0.5,(WIDTH//2)**-0.5,(WIDTH//4)**-0.5,WIDTH**-0.5,HIDDEN_SIZE**-0.5)
    for w in (0,3,4,1,2):
        at=7+3*w
        for i in range(3): loads[at+i].wait()
        if w==0:
            loads[6].wait()
            total=held[6]
            batch_grad=jnp.concatenate([total[0:4,:],total[4:8,:]],axis=1)
            grad=lax.dot_general(sig.astype(f32),batch_grad,(((0,),(0,)),((),())),precision=highest,preferred_element_type=f32)
        else:
            loads[1+w].wait()
            grad=held[1+w][...]
        master,first,second=held[at:at+3]
        first_new=beta_rate*first[...]+(1.0-beta_rate)*grad
        second_new=beta_rate*second[...]+(1.0-beta_rate)*grad*grad
        step=first_new/correct/(jnp.sqrt(second_new/correct)+adam_eps)
        old=master[...]
        master[...]=old-rates[w]*(step+weight_decay*old)
        first[...]=first_new
        second[...]=second_new
        for i in range(3): keep(held[at+i],2+3*w+i)
    for c in stores: c.wait()


def slots(neighbours, valid, node, rows):
    which=(neighbours//rows)^node
    slot=jnp.where(which==6,3,jnp.where((which==3)|(which==7),4,which))
    local=neighbours%rows
    spot=lax.broadcasted_iota(jnp.int32,neighbours.shape,0)%16
    hi=(slot*(rows//SPAN)+local//SPAN)*16+spot
    return jnp.where(valid>0,hi*256+local%SPAN,-1).reshape(-1,256)


def per_device_near(
    node_input, cotangent, sigma_embed, neighbours, neighbour_valid, batch_counts, step_count,
    ada_master, ada_first, ada_second, qkv_master, qkv_first, qkv_second, out_master, out_first, out_second,
    up_master, up_first, up_second, down_master, down_first, down_second,
):
    rows=node_input.shape[0]
    code=slots(neighbours,neighbour_valid,lax.axis_index("node"),rows)
    masters=(ada_master,qkv_master,out_master,up_master,down_master)
    firsts=(ada_first,qkv_first,out_first,up_first,down_first)
    seconds=(ada_second,qkv_second,out_second,up_second,down_second)
    V=pltpu.VMEM
    full=pl.BlockSpec(memory_space=V); few=pl.BlockSpec(memory_space=pltpu.SMEM); hbm=pl.BlockSpec(memory_space=pltpu.HBM)
    S=jax.ShapeDtypeStruct
    held=scratch(rows)
    sums=pl.pallas_call(functools.partial(layer_kernel,128**-0.5,tuple(held)),
        out_shape=(S((rows,512),bf16),S((4,rows//4,512),bf16))+tuple(S(a.shape,f32) for a in masters[1:])+(S((8,1024),f32),),
        in_specs=[full]*4+[few]+[full]*5,
        out_specs=(full,)*7,
        scratch_shapes=[V(*v) for v in held.values()]+[pltpu.SemaphoreType.DMA((COPIES,))]*2,
        compiler_params=pltpu.CompilerParams(vmem_limit_bytes=67043328,collective_id=1,has_side_effects=True),
        name="layer")(node_input,cotangent,sigma_embed,code,batch_counts,*masters)
    news=tuple(S(a.shape,f32) for a in masters for _ in range(3))
    inner=[V(a.shape,a.dtype) for a in sums]+[V(a.shape,f32) for a in masters for _ in range(3)]+[V((rows,512),f32)]
    return pl.pallas_call(finish_kernel,
        out_shape=(S((rows,512),bf16),S((rows,512),f32))+news,
        in_specs=[full,few]+[hbm]*(7+15),
        out_specs=(hbm,)*17,
        scratch_shapes=inner+[pltpu.SemaphoreType.DMA((22,)),pltpu.SemaphoreType.DMA((17,))],
        compiler_params=pltpu.CompilerParams(vmem_limit_bytes=67043328),
        name="finish")(sigma_embed,step_count,*sums,*[a for three in zip(masters,firsts,seconds) for a in three])


def wide_count_groups(cnt, hik, lok, rows):
    steps=hik.shape[0]
    parts=rows//SPAN
    total=5*parts*16
    rowid=lax.broadcasted_iota(jnp.int32,(total,1),0)
    rowkey=lax.div(rowid,16)*16+lax.rem(rowid,16)
    spot=lax.broadcasted_iota(jnp.int32,(SPAN,1),0)
    def body(g,_):
        keys=hik[pl.ds(g,1),:]
        low=lok[pl.ds(g,1),:]
        left=jnp.where(rowkey==keys,1.0,0.0).astype(bf16)
        right=jnp.where(spot==low,1.0,0.0).astype(bf16)
        made=lax.dot_general(left,right,NT,preferred_element_type=f32).astype(bf16)
        at=pl.multiple_of(g*16,16)
        for b in range(5):
            for p in range(parts):
                r=(b*parts+p)*16
                cnt[b,pl.ds(at,16),p*SPAN:(p+1)*SPAN]=made[r:r+16,:]
        return 0
    lax.fori_loop(0,steps,body,0)

def wide_add_self(cnt, block, rows):
    eye=(lax.broadcasted_iota(jnp.int32,(SPAN,SPAN),0)==lax.broadcasted_iota(jnp.int32,(SPAN,SPAN),1))
    one=jnp.where(eye,1.0,0.0).astype(bf16)
    for p in range(rows//SPAN):
        s=slice(p*SPAN,(p+1)*SPAN)
        cnt[block,s,s]=cnt[block,s,s]+one

def wide_attend_block(b, first, q, keys, vals, cnt, e, m, l, acc, fac, chunk, scale):
    rows=q.shape[0]
    lane=lax.broadcasted_iota(jnp.int32,(chunk,128),1)
    def body(i,_):
        at=pl.ds(pl.multiple_of(i*chunk,chunk),chunk)
        s=lax.dot_general(q[at,:],keys,NT,preferred_element_type=f32)*scale
        c=cnt[b,at,:].astype(f32)
        s=jnp.where(c>0,s,-1e30)
        top=jnp.max(s,axis=1,keepdims=True)
        if not first:
            old=m[at,0:1]
            top=jnp.maximum(top,old)
        w=(jnp.exp2(s-top)*c)
        total=jnp.sum(w,axis=1,keepdims=True)
        w=w.astype(bf16)
        e[b,at,:]=w
        out=jnp.dot(w,vals,preferred_element_type=f32)
        if first:
            acc[at,:]=out; l[at,:]=jnp.broadcast_to(total,(chunk,128))
            fac[at,:]=jnp.where(lane==b,top,0.0)
        else:
            shrink=jnp.exp2(old-top)
            acc[at,:]=acc[at,:]*shrink+out
            l[at,:]=l[at,:]*shrink+total
            fac[at,:]=jnp.where(lane==b,top,fac[at,:])
        m[at,:]=jnp.broadcast_to(top,(chunk,128))
        return 0
    lax.fori_loop(0,rows//chunk,body,0)

def wide_fwd_kernel(order, self_block, scale, q, kv, hik, lok, att, e, fac, cnt, m, l):
    rows=q.shape[0]
    wide_count_groups(cnt,hik,lok,rows)
    wide_add_self(cnt,self_block,rows)
    for t,b in enumerate(order):
        wide_attend_block(b,t==0,q,kv[b,:,:128],kv[b,:,128:],cnt,e,m,l,att,fac,256,scale)
    inv=1.0/l[...]
    att[...]=att[...]*inv
    fac[...]=jnp.exp2(fac[...]-m[...])*inv

def wide_attention_fwd(q,kv,hik,lok,scale):
    rows=q.shape[0]
    V=pltpu.VMEM
    full=pl.BlockSpec(memory_space=V)
    return pl.pallas_call(functools.partial(wide_fwd_kernel,(2,1,3,0,4),2,scale*math.log2(math.e)),
        out_shape=(jax.ShapeDtypeStruct((rows,128),f32),jax.ShapeDtypeStruct((5,rows,rows),bf16),jax.ShapeDtypeStruct((rows,128),f32)),
        in_specs=[full]*4,out_specs=(full,)*3,
        scratch_shapes=[V((5,rows,rows),bf16),V((rows,128),f32),V((rows,128),f32)],
        compiler_params=pltpu.CompilerParams(vmem_limit_bytes=60<<20),name="attend_fwd")(q,kv,hik,lok)

def wide_back_block(b, q_t, do, fac, delta, kv, e, dq, dkv, first, chunk, keyscale):
    rows=do.shape[0]
    f=fac[:,b:b+1]
    dob=(do*f)
    dobh=dob.astype(bf16)
    d=-(delta*f)
    h=d.astype(bf16); r=d-h.astype(f32); h2=r.astype(bf16); h3=(r-h2.astype(f32)).astype(bf16)
    lane=lax.broadcasted_iota(jnp.int32,(rows,128),1)
    zero=jnp.zeros((rows,128),bf16)
    dcol=jnp.where(lane==0,h.astype(f32),jnp.where(lane==1,h2.astype(f32),jnp.where(lane==2,h3.astype(f32),0.0))).astype(bf16)
    left=jnp.concatenate([dobh,dcol],axis=1)
    dob_t=dobh.T
    ones=jnp.ones((chunk,128),bf16)
    for i in range(kv.shape[1]//chunk):
        s=slice(i*chunk,(i+1)*chunk)
        right=jnp.concatenate([kv[b,s,128:],ones],axis=1)
        dp=lax.dot_general(left,right,NT,preferred_element_type=f32)
        w=e[b,:,s]
        ds=(dp*w.astype(f32)).astype(bf16)
        dkv[b,:128,s]=jnp.dot(q_t,ds,preferred_element_type=f32)*keyscale
        dkv[b,128:,s]=jnp.dot(dob_t,w,preferred_element_type=f32)
        out=jnp.dot(ds,kv[b,s,:128],preferred_element_type=f32)
        if first and i==0: dq[...]=out
        else: dq[...]+=out

def wide_bwd_kernel(scale, q, do, att, fac, kv, e, dq, dkv, ):
    q_t=q[...].T
    dof=do[...].astype(f32)
    delta=jnp.sum(dof*att[...],axis=1,keepdims=True)
    for t,b in enumerate((0,4,1,3,2)):
        wide_back_block(b,q_t,dof,fac,delta,kv,e,dq,dkv,t==0,512,scale)
    dq[...]=dq[...]*scale

def wide_attention_bwd(q,do,att,fac,kv,e,scale):
    rows=q.shape[0]
    V=pltpu.VMEM
    full=pl.BlockSpec(memory_space=V)
    return pl.pallas_call(functools.partial(wide_bwd_kernel,scale),
        out_shape=(jax.ShapeDtypeStruct((rows,128),f32),jax.ShapeDtypeStruct((5,256,rows),f32)),
        in_specs=[full]*6,out_specs=(full,)*2,
        compiler_params=pltpu.CompilerParams(vmem_limit_bytes=60<<20),name="attend_bwd")(q,do,att,fac,kv,e)

def wide_tables(slot_index, valid, rows):
    parts=rows//SPAN
    flat=slot_index.reshape(-1,256)
    ok=(valid>0).reshape(-1,256)
    node=lax.broadcasted_iota(jnp.int32,flat.shape,1)//16
    hi=jnp.where(ok,(flat//SPAN)*16+node,-1)
    lo=flat%SPAN
    return hi,lo


def per_device(
    node_input,
    cotangent,
    sigma_embed,
    neighbours,
    neighbour_valid,
    batch_counts,
    step_count,
    ada_master,
    ada_first,
    ada_second,
    qkv_master,
    qkv_first,
    qkv_second,
    out_master,
    out_first,
    out_second,
    up_master,
    up_first,
    up_second,
    down_master,
    down_first,
    down_second,
):
    f32 = jnp.float32
    bf16 = jnp.bfloat16
    node_rows = node_input.shape[0]
    model_width = node_input.shape[1]
    head_dim = qkv_master.shape[1] // 3
    score_scale = head_dim ** (-0.5)
    node_index = lax.axis_index("node")
    total_nodes = node_rows * lax.axis_size("node")
    qkv_full, out_full, up_full, down_full = (
        lax.all_gather(qkv_master.astype(bf16), "node", axis=0, tiled=True),
        lax.all_gather(out_master.astype(bf16), "node", axis=0, tiled=True),
        lax.all_gather(up_master.astype(bf16), "node", axis=0, tiled=True),
        lax.all_gather(down_master.astype(bf16), "node", axis=0, tiled=True),
    )
    cond_rows = ada_master.shape[0]
    sigma_part = lax.dynamic_slice_in_dim(sigma_embed, node_index * cond_rows, cond_rows, 1)
    limits = jnp.cumsum(batch_counts)[:-1]
    positions = node_index * node_rows + jnp.arange(node_rows, dtype=jnp.int32)
    member = jnp.sum((positions[:, None] >= limits[None, :]).astype(jnp.int32), axis=1)
    onehot = (
        member[:, None] == jnp.arange(batch_counts.shape[0], dtype=jnp.int32)[None, :]
    ).astype(f32)
    modulation = lax.psum(
        jnp.dot(sigma_part, ada_master.astype(bf16), preferred_element_type=f32), "node"
    )
    per_node = jnp.dot(onehot, modulation, precision=highest)
    scale_one = per_node[:, :model_width]
    shift_one = per_node[:, model_width : 2 * model_width]
    scale_two = per_node[:, 2 * model_width : 3 * model_width]
    shift_two = per_node[:, 3 * model_width :]
    normed_one, inverse_one = norm_parts(node_input.astype(f32))
    xn_one = (normed_one * (1.0 + scale_one) + shift_one).astype(bf16)
    projected = jnp.dot(xn_one, qkv_full, preferred_element_type=f32).astype(bf16)
    queries = projected[:, :head_dim]
    keys_values = projected[:, head_dim:]
    offsets = (-2, -1, 1, 2)
    fetched = {0: keys_values}
    for offset in offsets:
        fetched[offset] = passed_along(keys_values, "node", -offset)
    table = jnp.stack([fetched[offset] for offset in (-2, -1, 0, 1, 2)], axis=0)
    slot_index = jnp.mod(neighbours - (node_index - 2) * node_rows, total_nodes)
    high_keys, low_keys = wide_tables(slot_index, neighbour_valid, node_rows)
    mixed, weights, factors = wide_attention_fwd(queries, table, high_keys, low_keys, score_scale)
    heads_out = mixed.astype(bf16)
    branch = lax.psum(
        jnp.dot(heads_out, out_full, preferred_element_type=f32).astype(jnp.bfloat16), "head"
    ).astype(jnp.float32)
    middle = node_input.astype(f32) + branch
    normed_two, inverse_two = norm_parts(middle)
    xn_two = (normed_two * (1.0 + scale_two) + shift_two).astype(bf16)
    hidden_pre = jnp.dot(xn_two, up_full, preferred_element_type=f32)
    gate_sig = jax.nn.sigmoid(hidden_pre)
    activated = (hidden_pre * gate_sig).astype(bf16)
    mlp_sum = lax.psum(
        jnp.dot(activated, down_full, preferred_element_type=f32).astype(jnp.bfloat16), "head"
    ).astype(jnp.float32)
    node_output = (middle + mlp_sum).astype(bf16)
    down_grad = jnp.einsum("nf,nd->fd", activated, cotangent, preferred_element_type=f32)
    act_grad = jnp.einsum("nd,fd->nf", cotangent, down_full, preferred_element_type=f32)
    pre_grad = (act_grad * gate_sig * (1.0 + hidden_pre * (1.0 - gate_sig))).astype(bf16)
    up_grad = jnp.einsum("nw,nf->wf", xn_two, pre_grad, preferred_element_type=f32)
    normed_two_grad = lax.psum(
        jnp.einsum("nf,wf->nw", pre_grad, up_full, preferred_element_type=f32).astype(jnp.bfloat16),
        "head",
    ).astype(jnp.float32)
    middle_grad = cotangent.astype(f32) + norm_back(
        normed_two_grad * (1.0 + scale_two), normed_two, inverse_two
    )
    branch_grad = middle_grad.astype(bf16)
    out_grad = jnp.einsum("nh,nd->hd", heads_out, branch_grad, preferred_element_type=f32)
    mixed_grad = jnp.einsum("nd,hd->nh", branch_grad, out_full, preferred_element_type=f32).astype(
        bf16
    )
    query_grad, pair_sums = wide_attention_bwd(
        queries, mixed_grad, mixed, factors, table, weights, score_scale
    )
    remote_terms = pair_sums[2]
    for offset in offsets:
        remote_terms = remote_terms + passed_along(
            pair_sums[offset + 2].astype(bf16), "node", offset
        ).astype(f32)
    key_value_grad = remote_terms.T
    projected_grad = jnp.concatenate([query_grad, key_value_grad], axis=1).astype(bf16)
    qkv_grad = jnp.einsum("nw,nc->wc", xn_one, projected_grad, preferred_element_type=f32)
    normed_one_grad = lax.psum(
        jnp.einsum("nc,wc->nw", projected_grad, qkv_full, preferred_element_type=f32).astype(
            jnp.bfloat16
        ),
        "head",
    ).astype(jnp.float32)
    input_grad = middle_grad + norm_back(
        normed_one_grad * (1.0 + scale_one), normed_one, inverse_one
    )
    rows_grad = jnp.concatenate(
        [
            normed_one_grad * normed_one,
            normed_one_grad,
            normed_two_grad * normed_two,
            normed_two_grad,
        ],
        axis=1,
    )
    batch_grad = jnp.dot(onehot.T, rows_grad, precision=highest)
    batch_grad = lax.psum(batch_grad, "node")
    ada_sum = jnp.dot(sigma_part.astype(f32).T, batch_grad, precision=highest)
    qkv_sum, out_sum, up_sum, down_sum = (
        lax.psum_scatter(qkv_grad, "node", scatter_dimension=0, tiled=True),
        lax.psum_scatter(out_grad, "node", scatter_dimension=0, tiled=True),
        lax.psum_scatter(up_grad, "node", scatter_dimension=0, tiled=True),
        lax.psum_scatter(down_grad, "node", scatter_dimension=0, tiled=True),
    )
    count_value = step_count[0].astype(f32)
    ada_res = adamw_update(
        ada_master, ada_first, ada_second, ada_sum, (4 * COND) ** (-0.5), count_value
    )
    qkv_res = adamw_update(
        qkv_master, qkv_first, qkv_second, qkv_sum, (WIDTH // 2) ** (-0.5), count_value
    )
    out_res = adamw_update(
        out_master, out_first, out_second, out_sum, (WIDTH // 4) ** (-0.5), count_value
    )
    up_res = adamw_update(up_master, up_first, up_second, up_sum, WIDTH ** (-0.5), count_value)
    down_res = adamw_update(
        down_master, down_first, down_second, down_sum, HIDDEN_SIZE ** (-0.5), count_value
    )
    return (
        node_output,
        input_grad,
        ada_res[0],
        ada_res[1],
        ada_res[2],
        qkv_res[0],
        qkv_res[1],
        qkv_res[2],
        out_res[0],
        out_res[1],
        out_res[2],
        up_res[0],
        up_res[1],
        up_res[2],
        down_res[0],
        down_res[1],
        down_res[2],
    )


def solution(mesh):
    chosen = per_device_near if mesh.shape["node"] == 8 and mesh.shape["head"] == 4 else per_device
    placed = (
        P("node", None),
        P("node", None),
        P(),
        P("node", None),
        P("node", None),
        P(),
        P(),
        P("node", None),
        P("node", None),
        P("node", None),
        P("node", "head"),
        P("node", "head"),
        P("node", "head"),
        P(("head", "node"), None),
        P(("head", "node"), None),
        P(("head", "node"), None),
        P("node", "head"),
        P("node", "head"),
        P("node", "head"),
        P(("head", "node"), None),
        P(("head", "node"), None),
        P(("head", "node"), None),
    )
    return jax.shard_map(
        chosen,
        mesh=mesh,
        in_specs=placed,
        out_specs=(
            P("node", None),
            P("node", None),
            P("node", None),
            P("node", None),
            P("node", None),
            P("node", "head"),
            P("node", "head"),
            P("node", "head"),
            P(("head", "node"), None),
            P(("head", "node"), None),
            P(("head", "node"), None),
            P("node", "head"),
            P("node", "head"),
            P("node", "head"),
            P(("head", "node"), None),
            P(("head", "node"), None),
            P(("head", "node"), None),
        ),
        check_vma=False,
    )
```

profile of v0, /device:TPU:0, one launch (start us, length us, event | category | flops | bytes accessed | tf_op | source)
XLA Modules:
  0.0 169.1 jit_solution(16899501556683056095)
XLA Ops:
  1.3 1.0 fusion.6
  2.4 0.2 copy.40
  2.6 0.9 reshape.37.refs_3_
  3.4 159.1 %layer.1 = (bf16[1024,512]{1,0:T(8,128)(2,1)}, bf16[4,256,512]{2,1,0:T(8,128)(2,1)}, f32[64,384]{1,0:T(8,128)}, f32[16,512]{1,0:T(8,128)}, f32[64,512]{1,0:T(8,1...) custom-call(bf16[1024,512]{1,0:T(8,128)(2,1)} %refs_0_.1, bf16[1024,512]{1,0:T(8,128)(2,1)} %refs_1_.1, bf16[4,512]{1,0:T(4,128)(2,1)} %sigma.1, ...), custom_call_target="tpu_custom_call" | custom-call | tf_op jit(solution)/shard_map/layer/pallas_call | solution.py:538
  162.5 6.1 %finish.1 = (bf16[1024,512]{1,0:T(8,128)(2,1)}, f32[1024,512]{1,0:T(8,128)}, f32[64,2048]{1,0:T(8,128)}, f32[64,2048]{1,0:T(8,128)}, f32[64,2048]{1,0:T(8,128)},...) custom-call(bf16[4,512]{1,0:T(4,128)(2,1)} %sigma.1, ...), custom_call_target="tpu_custom_call" | custom-call | tf_op jit(solution)/shard_map/finish/pallas_call | solution.py:547
  (2 shorter events, 0.0 us)
where the time goes:
time: 172 us; the launch traced here: 169 us
  Pallas kernels  165 us (96%)
  between operations  1.8 us (1%)
    pallas_call x1, Pallas kernels, per_device_near(): pl.pallas_call(functools.partial(layer_kernel, 128 ** (-0.5), tuple(held)...  159 us
    pallas_call x1, Pallas kernels, per_device_near(): pl.pallas_call(finish_kernel, out_shape=(S((rows, 512), bf16), S((rows, 5...  6.13 us

commit v1 on v0

--- a/solution.py
+++ b/solution.py
@@ -165,6 +165,70 @@
     pl.semaphore_wait(barrier,len(peers))
 
 
+class Shown:
+    def __init__(self, links, head, node, place):
+        self.end=(head==0)|(head==3)
+        own=place(head)
+        self.two=links.go(own,own,head^2,node)
+        self.one=links.go(own,own,head^1,node)
+        self.three=links.copy(own,own,head^3,node)
+        pl.when(~self.end)(self.three.start)
+        far=place(jnp.where(self.end,head^3,head^2))
+        self.pass_copy=links.copy(far,far,head^1,node)
+
+    def onward(self):
+        @pl.when(~self.end)
+        def _():
+            self.two.wait_recv()
+            self.pass_copy.start()
+
+    def wait(self):
+        self.one.wait()
+        self.two.wait_send()
+        @pl.when(self.end)
+        def _():
+            self.two.wait_recv()
+            self.pass_copy.wait_recv()
+        @pl.when(~self.end)
+        def _():
+            self.three.wait()
+            self.pass_copy.wait_send()
+
+
+class Added:
+    def __init__(self, links, head, node, part, got, relay):
+        self.end=(head==0)|(head==3)
+        self.relay=relay
+        self.far=part(head^2)
+        self.zero=links.copy(part(head^3),relay,head^1,node)
+        self.two=links.copy(self.far,got(1),head^2,node)
+        self.one=links.copy(part(head^1),got(0),head^1,node)
+        self.three=links.copy(part(head^3),got(2),head^3,node)
+        @pl.when(self.end)
+        def _():
+            self.zero.start()
+            self.two.start()
+            self.one.start()
+            got(2)[...]=jnp.zeros(relay.shape,bf16)
+        @pl.when(~self.end)
+        def _():
+            self.three.start()
+            self.one.start()
+
+    def onward(self):
+        @pl.when(~self.end)
+        def _():
+            self.zero.wait_recv()
+            self.far[...]=summed(self.far,self.relay).astype(bf16)
+            self.two.start()
+
+    def wait(self):
+        pl.when(self.end)(self.zero.wait_send)
+        pl.when(~self.end)(self.three.wait)
+        self.one.wait()
+        self.two.wait()
+
+
 def wait_all(copies):
     for c in copies: c.wait()
 
@@ -174,8 +238,8 @@
 
 
 def summed(*refs):
-    total=refs[0].astype(f32)
-    for r in refs[1:]: total=total+r.astype(f32)
+    total=refs[0][...].astype(f32)
+    for r in refs[1:]: total=total+r[...].astype(f32)
     return total
 
 
@@ -190,15 +254,16 @@
         qkv_full=((512,384),bf16),out_full=((4,128,512),bf16),up_full=((512,2048),bf16),down_full=((4,512,512),bf16),
         modp=((8,1024),f32),modbuf=((8,8,1024),f32),modulation=((8,1024),f32),
         mixed=((rows,128),bf16),heads=((part,512),bf16),do=((rows,128),bf16),do_rows=((part,512),bf16),
-        act=((part,2048),bf16),pre=((part,2048),bf16),dy=((part,512),f32),out_rows=((part,512),bf16),
+        act=((part,2048),bf16),pre=((part,2048),bf16),dy=((part,512),f32),
         up_grad=((4,2,64,2048),bf16),down_grad=((4,4,2,64,512),bf16),out_grad=((4,4,2,16,512),bf16),
         dq=((rows,128),f32),dkv=((256,rows),f32),near=((5,256,rows),bf16),
         got_pair=((256,rows),bf16),got_y=((256,rows),bf16),got_x=((256,rows),bf16),got_one=((256,rows),bf16),
-        proj_grad=((rows,384),bf16),partial=((4,part,512),bf16),got_partial=((3,part,512),bf16),rows_grad=((part,512),bf16),normed=((rows,512),f32),
+        proj_grad=((rows,384),bf16),partial=((4,part,512),bf16),got_partial=((3,part,512),bf16),normed=((rows,512),f32),
         up1=((4,64,2048),bf16),down1=((4,4,64,512),bf16),out1=((4,4,16,512),bf16),
         up2=((2,64,2048),bf16),down2=((4,2,64,512),bf16),out2=((4,2,16,512),bf16),
         up3=((64,2048),bf16),down3=((4,64,512),bf16),out3=((4,16,512),bf16),
         up_z=((3,64,512),bf16),down_z=((3,64,512),bf16),out_z=((3,16,512),bf16),
+        up_relay=((64,512),bf16),down_relay=((64,512),bf16),out_relay=((16,512),bf16),relay=((part,512),bf16),
         qkv_grad=((8,64,384),bf16),qkv_got=((7,64,384),bf16),dm_own=((8,1024),f32),dm_z=((4,8,1024),f32),dm_n=((8,8,1024),f32),
     )
 
@@ -207,7 +272,7 @@
     pass
 
 
-COPIES=14+9+8+4+9+9+1+3+6+55
+COPIES=150
 
 
 def layer_kernel(scale, names, *refs):
@@ -248,9 +313,8 @@
         first.append(go(k.modp,k.modbuf.at[node],head,node^i))
         first.append(go(k.qkv_full.at[own],k.qkv_full.at[own],head,node^i))
     along=[]
-    for i in range(1,4):
-        for ref in (k.up_full.at[own,head_cols],k.down_full.at[head,own],k.out_full.at[head,own_out]):
-            along.append(go(ref,ref,head^i,node))
+    for place in (lambda h: k.up_full.at[own,block_of(h,512)],lambda h: k.down_full.at[h,own],lambda h: k.out_full.at[h,own_out]):
+        along.append(Shown(links,head,node,place))
     k.modbuf[node,:,:]=k.modp[...]
     for b in range(5): k.table[b,:,256:384]=jnp.ones((rows,128),bf16)
     def norm(i,_):
@@ -262,7 +326,8 @@
     lax.fori_loop(0,rows//256,norm,0)
     groups=code.shape[0]
     half=groups//2
-    count_groups(k.e,code,rows,0,half,8)
+    count_groups(k.e,code,rows,0,half,4)
+    for a in along: a.onward()
     wait_all(first)
     mod=k.modbuf[0]
     for i in range(1,8): mod=mod+k.modbuf[i]
@@ -279,7 +344,7 @@
         k.table[0,at,kv]=proj[:,128:]
         across.append(go(k.table.at[0,at,kv],k.table.at[2,at,kv],head,node^2))
         paired.append(go(k.table.at[0,at,kv],k.table.at[1,at,kv],head,node^1))
-    count_groups(k.e,code,rows,half,groups,8)
+    count_groups(k.e,code,rows,half,groups,4)
     add_self(k.e,0,rows)
 
     onward=[]
@@ -359,7 +424,7 @@
     for i in range(1,4):
         returned.append(go(k.do_rows.at[:,block_of(head^i,128)],k.do.at[mine],head^i,node))
     k.do[mine,:]=k.do_rows[:,lanes]
-    k.out_rows[...]=(y+mlp).astype(bf16)
+    node_output[mine,:]=(y+mlp).astype(bf16)
     xn_t=xn.T
     heads_t=k.heads[...].T
     k.out_grad[...]=jnp.dot(heads_t,da,preferred_element_type=f32).astype(bf16).reshape(4,4,2,16,512)
@@ -371,8 +436,7 @@
     k.dm_own[4:8,0:512]=batch_sums(own_pos,limits,dxn*n_two)
     k.dm_own[4:8,512:1024]=batch_sums(own_pos,limits,dxn)
     wait_all(returned)
-    shown=[go(k.out_rows,node_output.at[mine],head^i,node) for i in range(1,4)]
-    node_output[mine,:]=k.out_rows[...]
+    shown=Shown(links,head,node,lambda h: node_output.at[block_of(h,part)])
 
     q_t=k.queries[...].T
     dof=k.do[...].astype(f32)
@@ -400,6 +464,7 @@
         near[2,:,s]=summed(near[2,:,s],k.got_y[:,s]).astype(bf16)
         via_x.append(go(near.at[2,:,s],k.got_x.at[:,s],head,node^2))
     pass_on(0)
+    shown.onward()
     block(1)
     one=go(near.at[1],k.got_one,head,node^1)
     pass_on(1)
@@ -423,9 +488,10 @@
         k.proj_grad[s,128:]=total.T.astype(bf16)
         k.proj_grad[s,:128]=(k.dq[s,:]*scale).astype(bf16)
         k.partial[i]=lax.dot_general(k.proj_grad[s,:],k.qkv_full[...],NT,preferred_element_type=f32).astype(bf16)
-    reduce=[go(k.partial.at[head^i],k.got_partial.at[i-1],head^i,node) for i in range(1,4)]
+    reduce=Added(links,head,node,lambda h: k.partial.at[h],lambda i: k.got_partial.at[i],k.relay)
     k.qkv_grad[...]=jnp.dot(xn_t,k.proj_grad[...],preferred_element_type=f32).astype(bf16).reshape(8,64,384)
     qkv_moves=[go(k.qkv_grad.at[node^i],k.qkv_got.at[i-1],head,node^i) for i in range(1,8)]
+    reduce.onward()
     wait_all(stage2)
     for i in range(2):
         k.up2[i]=summed(k.up2[i],k.up1[i*2+x_at]).astype(bf16)
@@ -441,22 +507,23 @@
     k.up3[...]=summed(k.up3[...],k.up2[y_at]).astype(bf16)
     k.down3[...]=summed(k.down3[...],k.down2[:,x_at]).astype(bf16)
     k.out3[...]=summed(k.out3[...],k.out2[:,x_at]).astype(bf16)
-    wait_all(reduce)
-    dxn=summed(k.partial[head],*[k.got_partial[i] for i in range(3)])
-    k.rows_grad[...]=(k.dy[...]+norm_back(dxn*scale_one,n_one,inv_one)).astype(bf16)
-    spread=[go(k.rows_grad,row_all.at[head],head^i,node) for i in range(1,4)]
-    row_all[head,:,:]=k.rows_grad[...]
+    stage4=[Added(links,head,node,lambda h: k.up3.at[:,block_of(h,512)],lambda i: k.up_z.at[i],k.up_relay),
+        Added(links,head,node,lambda h: k.down3.at[h],lambda i: k.down_z.at[i],k.down_relay),
+        Added(links,head,node,lambda h: k.out3.at[h],lambda i: k.out_z.at[i],k.out_relay)]
+    reduce.wait()
+    dxn=summed(k.partial.at[head],*[k.got_partial.at[i] for i in range(3)])
     k.dm_own[0:4,0:512]=batch_sums(own_pos,limits,dxn*n_one)
     k.dm_own[0:4,512:1024]=batch_sums(own_pos,limits,dxn)
     dm_moves=[go(k.dm_own,k.dm_z.at[head],head^i,node) for i in range(1,4)]
+    row_all[head,:,:]=(k.dy[...]+norm_back(dxn*scale_one,n_one,inv_one)).astype(bf16)
+    spread=Shown(links,head,node,lambda h: row_all.at[h])
+    for s in stage4: s.onward()
     k.dm_z[head,:,:]=k.dm_own[...]
-    stage4=[]
-    for i in range(1,4):
-        stage4+=[go(k.up3.at[:,block_of(head^i,512)],k.up_z.at[i-1],head^i,node),go(k.down3.at[head^i],k.down_z.at[i-1],head^i,node),go(k.out3.at[head^i],k.out_z.at[i-1],head^i,node)]
     wait_all(dm_moves)
     k.modp[...]=k.dm_z[0]+k.dm_z[1]+k.dm_z[2]+k.dm_z[3]
     dm_last=[go(k.modp,k.dm_n.at[node],head,node^i) for i in range(1,8)]
     k.dm_n[node,:,:]=k.modp[...]
+    spread.onward()
     wait_all(dm_last)
     total=k.dm_n[0]
     for i in range(1,8): total=total+k.dm_n[i]
@@ -465,8 +532,8 @@
     up_sum[...]=summed(k.up3[:,head_cols],*[k.up_z[i] for i in range(3)])
     down_sum[...]=summed(k.down3[head],*[k.down_z[i] for i in range(3)])
     out_sum[...]=summed(k.out3[head],*[k.out_z[i] for i in range(3)])
-    wait_all(spread)
-    wait_all(shown)
+    spread.wait()
+    shown.wait()
 
 
 def finish_kernel(sigma, step_count, *refs):

time: 172 us -> 162 us (0.942)
  Pallas kernels: 165 us -> 155 us
    pallas_call x1, Pallas kernels: 159 us -> 149 us  [per_device_near(): pl.pallas_call(functools.partial(layer_kernel, 128 ** (-0.5), tuple(held)...]
where the time goes in v1:
time: 162 us; the launch traced here: 159 us
  Pallas kernels  155 us (96%)
  between operations  1.8 us (1%)
    pallas_call x1, Pallas kernels, per_device_near(): pl.pallas_call(functools.partial(layer_kernel, 128 ** (-0.5), tuple(held)...  149 us
    pallas_call x1, Pallas kernels, per_device_near(): pl.pallas_call(finish_kernel, out_shape=(S((rows, 512), bf16), S((rows, 5...  6.12 us

profile of v1, /device:TPU:0, one launch (start us, length us, event | category | flops | bytes accessed | tf_op | source)
XLA Modules:
  0.0 158.6 jit_solution(14061389357338760124)
XLA Ops:
  1.3 1.0 fusion.6
  2.4 0.2 copy.40
  2.6 0.9 reshape.37.refs_3_
  3.4 148.6 %layer.1 = (bf16[1024,512]{1,0:T(8,128)(2,1)}, bf16[4,256,512]{2,1,0:T(8,128)(2,1)}, f32[64,384]{1,0:T(8,128)}, f32[16,512]{1,0:T(8,128)}, f32[64,512]{1,0:T(8,1...) custom-call(bf16[1024,512]{1,0:T(8,128)(2,1)} %refs_0_.1, bf16[1024,512]{1,0:T(8,128)(2,1)} %refs_1_.1, bf16[4,512]{1,0:T(4,128)(2,1)} %sigma.1, ...), custom_call_target="tpu_custom_call" | custom-call | tf_op jit(solution)/shard_map/layer/pallas_call | solution.py:605
  152.0 6.1 %finish.1 = (bf16[1024,512]{1,0:T(8,128)(2,1)}, f32[1024,512]{1,0:T(8,128)}, f32[64,2048]{1,0:T(8,128)}, f32[64,2048]{1,0:T(8,128)}, f32[64,2048]{1,0:T(8,128)},...) custom-call(bf16[4,512]{1,0:T(4,128)(2,1)} %sigma.1, ...), custom_call_target="tpu_custom_call" | custom-call | tf_op jit(solution)/shard_map/finish/pallas_call | solution.py:614
  (2 shorter events, 0.0 us)

commit v2 on v1

--- a/solution.py
+++ b/solution.py
@@ -83,8 +83,7 @@
         s=slice(p*SPAN,(p+1)*SPAN)
         cnt[block,s,s]=cnt[block,s,s]+one
 
-def attend_rows(b, first, at, q, table, e, m, l, acc, fac, scale):
-    size=at.stop-at.start
+def attend_rows(b, first, at, size, q, table, e, m, l, acc, fac, scale):
     lane=lax.broadcasted_iota(jnp.int32,(size,128),1)
     s=lax.dot_general(q[at,:],table[b,:,0:128],NT,preferred_element_type=f32)*scale
     c=e[b,at,:].astype(f32)
@@ -328,6 +327,12 @@
     half=groups//2
     count_groups(k.e,code,rows,0,half,4)
     for a in along: a.onward()
+    def column(which):
+        at=block_of(node^which,64)
+        return [k.up_full.at[at],k.down_full.at[:,at],k.out_full.at[:,block_of(node^which,16)]]
+    own_column=column(0); from_x=column(2); from_y=column(4)
+    along[0].wait()
+    up_x=go(own_column[0],own_column[0],head,node^2)
     wait_all(first)
     mod=k.modbuf[0]
     for i in range(1,8): mod=mod+k.modbuf[i]
@@ -344,6 +349,8 @@
         k.table[0,at,kv]=proj[:,128:]
         across.append(go(k.table.at[0,at,kv],k.table.at[2,at,kv],head,node^2))
         paired.append(go(k.table.at[0,at,kv],k.table.at[1,at,kv],head,node^1))
+    wait_all(along[1:])
+    rest_y=[go(r,r,head,node^4) for r in own_column[1:]]
     count_groups(k.e,code,rows,half,groups,4)
     add_self(k.e,0,rows)
 
@@ -353,23 +360,27 @@
         across[i].wait_recv()
         onward.append(go(k.table.at[2,at,kv],k.table.at[3,at,kv],head,node^4))
     def attend(b,at):
-        attend_rows(b,b==0,at,k.queries,k.table,k.e,k.m,k.l,k.att,k.fac,scale*math.log2(math.e))
-    def column(which):
-        at=block_of(node^which,64)
-        return [k.up_full.at[at],k.down_full.at[:,at],k.out_full.at[:,block_of(node^which,16)]]
+        attend_rows(b,b==0,at,part,k.queries,k.table,k.e,k.m,k.l,k.att,k.fac,scale*math.log2(math.e))
+    def attend_all(b):
+        def two(i,_):
+            for u in range(2): attend(b,block_of(2*i+u,part))
+            return 0
+        lax.fori_loop(0,2,two,0)
     pass_keys(0)
-    for at in quarter: attend(0,at)
+    attend_all(0)
     pass_keys(1)
     wait_all(paired)
-    for at in quarter: attend(1,at)
+    attend_all(1)
     pass_keys(2)
     pass_keys(3)
-    wait_all(along)
-    own_column=column(0)
-    to_x=[go(r,r,head,node^2) for r in own_column]
-    to_y=[go(r,r,head,node^4) for r in own_column]
+    up_y=go(own_column[0],own_column[0],head,node^4)
+    rest_x=[go(r,r,head,node^2) for r in own_column[1:]]
     to_pair=[go(r,r,head,node^1) for r in own_column]
-    for at in quarter: attend(2,at)
+    up_x.wait()
+    wait_all(rest_y)
+    cross=[go(from_x[0],from_x[0],head,node^4)]+[go(r,r,head,node^2) for r in from_y[1:]]
+    hand=[go(r,r,head,node^1) for r in from_x[:1]+from_y[1:]]
+    attend_all(2)
     wait_all(onward)
     fifth=go(k.table.at[jnp.where(x_at==core,2,3),:,kv],k.table.at[4,:,kv],head,node^1)
     for at in quarter: attend(3,at)
@@ -388,10 +399,9 @@
         moved.append(go(k.mixed.at[block_of(head^i,part)],k.heads.at[:,lanes],head^i,node))
     k.heads[:,lanes]=k.mixed[mine,:]
     for c in across: c.wait_send()
-    wait_all(to_x+to_y)
-    from_x=column(2); from_y=column(4)
-    cross=[go(from_x[0],from_x[0],head,node^4)]+[go(r,r,head,node^2) for r in from_y[1:]]
-    hand=[go(r,r,head,node^1) for r in from_x+from_y]
+    up_y.wait()
+    wait_all(rest_x)
+    hand+=[go(r,r,head,node^1) for r in from_y[:1]+from_x[1:]]
     wait_all(cross)
     last=[go(r,r,head,node^1) for r in column(6)]
     scale_two=1.0+by_batch(own_pos,limits,k.modulation,4,slice(0,512))

time: 162 us -> 157 us (0.969); the launches traced: 159 us -> 157 us
  Pallas kernels: 155 us -> 153 us
where the time goes in v2:
time: 157 us
  Pallas kernels  153 us (97%)
    pallas_call x1, Pallas kernels, per_device_near(): pl.pallas_call(functools.partial(layer_kernel, 128 ** (-0.5), tuple(held)...  147 us
    pallas_call x1, Pallas kernels, per_device_near(): pl.pallas_call(finish_kernel, out_shape=(S((rows, 512), bf16), S((rows, 5...  6.13 us

profile of v2, /device:TPU:0, one launch (start us, length us, event | category | flops | bytes accessed | tf_op | source)
XLA Modules:
  0.0 156.7 jit_solution(15309205866510466126)
XLA Ops:
  1.3 1.0 fusion.6
  2.4 0.2 copy.40
  2.6 0.9 reshape.37.refs_3_
  3.4 147.0 %layer.1 = (bf16[1024,512]{1,0:T(8,128)(2,1)}, bf16[4,256,512]{2,1,0:T(8,128)(2,1)}, f32[64,384]{1,0:T(8,128)}, f32[16,512]{1,0:T(8,128)}, f32[64,512]{1,0:T(8,1...) custom-call(bf16[1024,512]{1,0:T(8,128)(2,1)} %refs_0_.1, bf16[1024,512]{1,0:T(8,128)(2,1)} %refs_1_.1, bf16[4,512]{1,0:T(4,128)(2,1)} %sigma.1, ...), custom_call_target="tpu_custom_call" | custom-call | tf_op jit(solution)/shard_map/layer/pallas_call | solution.py:615
  150.4 6.1 %finish.1 = (bf16[1024,512]{1,0:T(8,128)(2,1)}, f32[1024,512]{1,0:T(8,128)}, f32[64,2048]{1,0:T(8,128)}, f32[64,2048]{1,0:T(8,128)}, f32[64,2048]{1,0:T(8,128)},...) custom-call(bf16[4,512]{1,0:T(4,128)(2,1)} %sigma.1, ...), custom_call_target="tpu_custom_call" | custom-call | tf_op jit(solution)/shard_map/finish/pallas_call | solution.py:624
  (2 shorter events, 0.0 us)

commit v3 on v2

--- a/solution.py
+++ b/solution.py
@@ -203,16 +203,27 @@
         self.two=links.copy(self.far,got(1),head^2,node)
         self.one=links.copy(part(head^1),got(0),head^1,node)
         self.three=links.copy(part(head^3),got(2),head^3,node)
+        self.head=head
+        @pl.when(self.end)
+        def _(): got(2)[...]=jnp.zeros(relay.shape,bf16)
+
+    def begin(self, to):
+        pl.when(self.end&(self.head==to^3))(self.zero.start)
+        pl.when((~self.end)&(self.head==to^3))(self.three.start)
+        pl.when(self.end&(self.head==to^2))(self.two.start)
+        pl.when(self.head==to^1)(self.one.start)
+
+    def begin_all(self):
         @pl.when(self.end)
         def _():
             self.zero.start()
             self.two.start()
             self.one.start()
-            got(2)[...]=jnp.zeros(relay.shape,bf16)
         @pl.when(~self.end)
         def _():
             self.three.start()
             self.one.start()
+        return self
 
     def onward(self):
         @pl.when(~self.end)
@@ -463,42 +474,49 @@
     give.wait()
     @pl.when(x_at!=core)
     def _(): near[3]=summed(near[3],k.got_pair[...]).astype(bf16)
-    via_y=[go(near.at[3,:,s],k.got_y.at[:,s],head,node^4) for s in quarter]
+    order=(0,3,1,2)
+    via_y={i:go(near.at[3,:,quarter[i]],k.got_y.at[:,quarter[i]],head,node^4) for i in order}
     block(2)
     @pl.when(x_at==core)
     def _(): near[2]=summed(near[2],k.got_pair[...]).astype(bf16)
-    via_x=[]
+    via_x={}
     def pass_on(i):
+        i=order[i]
         s=quarter[i]
         via_y[i].wait()
         near[2,:,s]=summed(near[2,:,s],k.got_y[:,s]).astype(bf16)
-        via_x.append(go(near.at[2,:,s],k.got_x.at[:,s],head,node^2))
+        via_x[i]=go(near.at[2,:,s],k.got_x.at[:,s],head,node^2)
     pass_on(0)
     shown.onward()
     block(1)
     one=go(near.at[1],k.got_one,head,node^1)
     pass_on(1)
-    pass_on(2)
     block(0)
-    pass_on(3)
     wait_all(stage1)
     for i in range(4):
-        k.up1[i]=summed(k.up1[i],k.up_grad[i,core]).astype(bf16)
         k.down1[i]=summed(k.down1[i],k.down_grad[i,:,core]).astype(bf16)
         k.out1[i]=summed(k.out1[i],k.out_grad[i,:,core]).astype(bf16)
-    stage2=[go(k.up1.at[i*2+1-x_at],k.up2.at[i],head,node^2) for i in range(2)]
     there=pl.ds((1-y_at)*2,2)
-    stage2+=[go(k.down1.at[:,there],k.down2,head,node^4),go(k.out1.at[:,there],k.out2,head,node^4)]
-    xn_t=k.xn_one[...].T
+    stage2=[go(k.down1.at[:,there],k.down2,head,node^4),go(k.out1.at[:,there],k.out2,head,node^4)]
+    pass_on(2)
     one.wait()
-    for i in range(4):
+    reduce=Added(links,head,node,lambda h: k.partial.at[h],lambda i: k.got_partial.at[i],k.relay)
+    def finish_rows(i):
+        i=order[i]
         s=quarter[i]
         via_x[i].wait()
         total=k.dkv[:,s]+k.got_one[:,s].astype(f32)+k.got_x[:,s].astype(f32)
         k.proj_grad[s,128:]=total.T.astype(bf16)
         k.proj_grad[s,:128]=(k.dq[s,:]*scale).astype(bf16)
         k.partial[i]=lax.dot_general(k.proj_grad[s,:],k.qkv_full[...],NT,preferred_element_type=f32).astype(bf16)
-    reduce=Added(links,head,node,lambda h: k.partial.at[h],lambda i: k.got_partial.at[i],k.relay)
+        reduce.begin(i)
+    finish_rows(0)
+    pass_on(3)
+    for i in range(4):
+        k.up1[i]=summed(k.up1[i],k.up_grad[i,core]).astype(bf16)
+    stage2+=[go(k.up1.at[i*2+1-x_at],k.up2.at[i],head,node^2) for i in range(2)]
+    for i in range(1,4): finish_rows(i)
+    xn_t=k.xn_one[...].T
     k.qkv_grad[...]=jnp.dot(xn_t,k.proj_grad[...],preferred_element_type=f32).astype(bf16).reshape(8,64,384)
     qkv_moves=[go(k.qkv_grad.at[node^i],k.qkv_got.at[i-1],head,node^i) for i in range(1,8)]
     reduce.onward()
@@ -511,15 +529,6 @@
     stage3=[go(k.up2.at[1-y_at],k.up3,head,node^4),go(k.down2.at[:,1-x_at],k.down3,head,node^2),go(k.out2.at[:,1-x_at],k.out3,head,node^2)]
     scale_one=1.0+by_batch(own_pos,limits,k.modulation,0,slice(0,512))
     n_one,inv_one=norm_parts(node_input[mine,:].astype(f32))
-    wait_all(qkv_moves)
-    qkv_sum[...]=summed(k.qkv_grad[node],*[k.qkv_got[i] for i in range(7)])
-    wait_all(stage3)
-    k.up3[...]=summed(k.up3[...],k.up2[y_at]).astype(bf16)
-    k.down3[...]=summed(k.down3[...],k.down2[:,x_at]).astype(bf16)
-    k.out3[...]=summed(k.out3[...],k.out2[:,x_at]).astype(bf16)
-    stage4=[Added(links,head,node,lambda h: k.up3.at[:,block_of(h,512)],lambda i: k.up_z.at[i],k.up_relay),
-        Added(links,head,node,lambda h: k.down3.at[h],lambda i: k.down_z.at[i],k.down_relay),
-        Added(links,head,node,lambda h: k.out3.at[h],lambda i: k.out_z.at[i],k.out_relay)]
     reduce.wait()
     dxn=summed(k.partial.at[head],*[k.got_partial.at[i] for i in range(3)])
     k.dm_own[0:4,0:512]=batch_sums(own_pos,limits,dxn*n_one)
@@ -527,13 +536,22 @@
     dm_moves=[go(k.dm_own,k.dm_z.at[head],head^i,node) for i in range(1,4)]
     row_all[head,:,:]=(k.dy[...]+norm_back(dxn*scale_one,n_one,inv_one)).astype(bf16)
     spread=Shown(links,head,node,lambda h: row_all.at[h])
+    wait_all(qkv_moves)
+    qkv_sum[...]=summed(k.qkv_grad[node],*[k.qkv_got[i] for i in range(7)])
+    wait_all(stage3)
+    k.up3[...]=summed(k.up3[...],k.up2[y_at]).astype(bf16)
+    k.down3[...]=summed(k.down3[...],k.down2[:,x_at]).astype(bf16)
+    k.out3[...]=summed(k.out3[...],k.out2[:,x_at]).astype(bf16)
+    stage4=[Added(links,head,node,lambda h: k.up3.at[:,block_of(h,512)],lambda i: k.up_z.at[i],k.up_relay).begin_all(),
+        Added(links,head,node,lambda h: k.down3.at[h],lambda i: k.down_z.at[i],k.down_relay).begin_all(),
+        Added(links,head,node,lambda h: k.out3.at[h],lambda i: k.out_z.at[i],k.out_relay).begin_all()]
+    spread.onward()
     for s in stage4: s.onward()
     k.dm_z[head,:,:]=k.dm_own[...]
     wait_all(dm_moves)
     k.modp[...]=k.dm_z[0]+k.dm_z[1]+k.dm_z[2]+k.dm_z[3]
     dm_last=[go(k.modp,k.dm_n.at[node],head,node^i) for i in range(1,8)]
     k.dm_n[node,:,:]=k.modp[...]
-    spread.onward()
     wait_all(dm_last)
     total=k.dm_n[0]
     for i in range(1,8): total=total+k.dm_n[i]

time: 157 us -> 149 us (0.949)
  Pallas kernels: 153 us -> 146 us
    pallas_call x1, Pallas kernels: 147 us -> 139 us  [per_device_near(): pl.pallas_call(functools.partial(layer_kernel, 128 ** (-0.5), tuple(held)...]
where the time goes in v3:
time: 149 us
  Pallas kernels  146 us (98%)
  between operations  1.53 us (1%)
    pallas_call x1, Pallas kernels, per_device_near(): pl.pallas_call(functools.partial(layer_kernel, 128 ** (-0.5), tuple(held)...  139 us
    pallas_call x1, Pallas kernels, per_device_near(): pl.pallas_call(finish_kernel, out_shape=(S((rows, 512), bf16), S((rows, 5...  6.12 us

profile of v3, /device:TPU:0, one launch (start us, length us, event | category | flops | bytes accessed | tf_op | source)
XLA Modules:
  0.0 149.2 jit_solution(1446517801853154789)
XLA Ops:
  1.3 1.0 fusion.6
  2.4 0.2 copy.40
  2.6 0.9 reshape.37.refs_3_
  3.4 139.5 %layer.1 = (bf16[1024,512]{1,0:T(8,128)(2,1)}, bf16[4,256,512]{2,1,0:T(8,128)(2,1)}, f32[64,384]{1,0:T(8,128)}, f32[16,512]{1,0:T(8,128)}, f32[64,512]{1,0:T(8,1...) custom-call(bf16[1024,512]{1,0:T(8,128)(2,1)} %refs_0_.1, bf16[1024,512]{1,0:T(8,128)(2,1)} %refs_1_.1, bf16[4,512]{1,0:T(4,128)(2,1)} %sigma.1, ...), custom_call_target="tpu_custom_call" | custom-call | tf_op jit(solution)/shard_map/layer/pallas_call | solution.py:633
  142.9 6.1 %finish.1 = (bf16[1024,512]{1,0:T(8,128)(2,1)}, f32[1024,512]{1,0:T(8,128)}, f32[64,2048]{1,0:T(8,128)}, f32[64,2048]{1,0:T(8,128)}, f32[64,2048]{1,0:T(8,128)},...) custom-call(bf16[4,512]{1,0:T(4,128)(2,1)} %sigma.1, ...), custom_call_target="tpu_custom_call" | custom-call | tf_op jit(solution)/shard_map/finish/pallas_call | solution.py:642
  (2 shorter events, 0.0 us)

commit v4 on v3

--- a/solution.py
+++ b/solution.py
@@ -531,11 +531,11 @@
     n_one,inv_one=norm_parts(node_input[mine,:].astype(f32))
     reduce.wait()
     dxn=summed(k.partial.at[head],*[k.got_partial.at[i] for i in range(3)])
+    row_all[head,:,:]=(k.dy[...]+norm_back(dxn*scale_one,n_one,inv_one)).astype(bf16)
+    spread=Shown(links,head,node,lambda h: row_all.at[h])
     k.dm_own[0:4,0:512]=batch_sums(own_pos,limits,dxn*n_one)
     k.dm_own[0:4,512:1024]=batch_sums(own_pos,limits,dxn)
     dm_moves=[go(k.dm_own,k.dm_z.at[head],head^i,node) for i in range(1,4)]
-    row_all[head,:,:]=(k.dy[...]+norm_back(dxn*scale_one,n_one,inv_one)).astype(bf16)
-    spread=Shown(links,head,node,lambda h: row_all.at[h])
     wait_all(qkv_moves)
     qkv_sum[...]=summed(k.qkv_grad[node],*[k.qkv_got[i] for i in range(7)])
     wait_all(stage3)

time: 149 us -> 150 us (level)
  no operation moved by 1% of the time
where the time goes in v4:
time: 150 us; the launch traced here: 149 us
  Pallas kernels  146 us (97%)
  between operations  1.53 us (1%)
    pallas_call x1, Pallas kernels, per_device_near(): pl.pallas_call(functools.partial(layer_kernel, 128 ** (-0.5), tuple(held)...  140 us
    pallas_call x1, Pallas kernels, per_device_near(): pl.pallas_call(finish_kernel, out_shape=(S((rows, 512), bf16), S((rows, 5...  6.12 us

profile of v4, /device:TPU:0, one launch (start us, length us, event | category | flops | bytes accessed | tf_op | source)
XLA Modules:
  0.0 149.3 jit_solution(3490515741807534299)
XLA Ops:
  1.3 1.0 fusion.6
  2.4 0.2 copy.40
  2.6 0.9 reshape.37.refs_3_
  3.4 139.6 %layer.1 = (bf16[1024,512]{1,0:T(8,128)(2,1)}, bf16[4,256,512]{2,1,0:T(8,128)(2,1)}, f32[64,384]{1,0:T(8,128)}, f32[16,512]{1,0:T(8,128)}, f32[64,512]{1,0:T(8,1...) custom-call(bf16[1024,512]{1,0:T(8,128)(2,1)} %refs_0_.1, bf16[1024,512]{1,0:T(8,128)(2,1)} %refs_1_.1, bf16[4,512]{1,0:T(4,128)(2,1)} %sigma.1, ...), custom_call_target="tpu_custom_call" | custom-call | tf_op jit(solution)/shard_map/layer/pallas_call | solution.py:633
  143.0 6.1 %finish.1 = (bf16[1024,512]{1,0:T(8,128)(2,1)}, f32[1024,512]{1,0:T(8,128)}, f32[64,2048]{1,0:T(8,128)}, f32[64,2048]{1,0:T(8,128)}, f32[64,2048]{1,0:T(8,128)},...) custom-call(bf16[4,512]{1,0:T(4,128)(2,1)} %sigma.1, ...), custom_call_target="tpu_custom_call" | custom-call | tf_op jit(solution)/shard_map/finish/pallas_call | solution.py:642
  (2 shorter events, 0.0 us)
